TPU v7x, 512 devices: a whole 4x4x16 slice. The times are simulated.
512 devices in a mesh: depth: 64 (over y, z_lo, core), freq: 8 (over x, z_hi).
Axes of the slice: x: 4, y: 4, z: 16 (z_hi: 2, z_lo: 8; z = z_hi * 8 + z_lo), core: 2. Of those that a mesh axis runs over, the one named last changes fastest.
Arguments:
- extrapolation_operator: float32 [8, 64, 2, 512, 512], P('freq', 'depth'), may hold values from -0.1875 to 0.1875
- impedance_contrast: float32 [64, 512], P('depth'), may hold values from -3 to 3
- ascending_residual: float32 [8, 64, 5, 2, 96, 512], P('freq', 'depth'), may hold values from -6 to 6
- arriving_downward_matrices: float32 [8, 64, 2, 96, 512], P('freq', 'depth'), may hold values from -6 to 6
- shot_node_indices: int32 [4, 96], replicated, may hold values from 0 to 511
- emitted_pulse: float32 [8, 4, 2], P('freq'), may hold values from -4 to 4
Outputs:
- departing_downward_matrices: float32 [8, 64, 2, 96, 512], P('freq', 'depth')
- gradient: float32 [64, 512], P('depth', 'freq')
All inputs are finite; a program needn't handle non-finite values.
Results may differ from a plain program's by a relative error of at most 0.00013.
Values sent between devices are 32-bit elements; how exact they have to be, the bound alone decides.
A program may use at most 64 MiB of HBM per device.

v0:
```python
import math

import jax
import jax.numpy as jnp
from jax import lax
from jax.sharding import PartitionSpec as P

TICKS = 5


def from_behind(block, axis, distance):
    devices = range(lax.axis_size(axis))
    route = [(i - distance, i) for i in devices if i - distance in devices]
    return lax.ppermute(block, axis, route)


def matmul_high(left, right):
    return jnp.dot(left, right, precision=lax.Precision.HIGHEST, preferred_element_type=jnp.float32)


def local(
    extrapolation_operator,
    impedance_contrast,
    ascending_residual,
    arriving_downward_matrices,
    shot_node_indices,
    emitted_pulse,
):
    prop_real = extrapolation_operator[0, 0, 0]
    prop_imag = extrapolation_operator[0, 0, 1]
    reflect = impedance_contrast[0]
    shot_matrix = arriving_downward_matrices.shape[3]
    shot_matrix_breadth = arriving_downward_matrices.shape[4]
    at_surface = lax.axis_index("depth") == 0
    columns = jnp.arange(shot_matrix_breadth, dtype=jnp.int32)
    grad_scale = 1.0 / math.sqrt(shot_matrix * TICKS)
    present_shot_matrix = arriving_downward_matrices[0, 0]
    gradient_sum = jnp.zeros((shot_matrix_breadth,), jnp.float32)
    outgoing = present_shot_matrix
    for moment in range(TICKS):
        wave_now = ascending_residual[0, 0, moment]
        grad_term = jnp.sum(present_shot_matrix * wave_now, axis=(0, 1)) * grad_scale
        gradient_sum = gradient_sum + grad_term
        sending = moment < TICKS - 1
        mixed = present_shot_matrix + reflect[None, None, :] * wave_now
        real_out = matmul_high(mixed[0], prop_real) - matmul_high(mixed[1], prop_imag)
        imag_out = matmul_high(mixed[0], prop_imag) + matmul_high(mixed[1], prop_real)
        outgoing = jnp.stack([real_out, imag_out], 0)
        if sending:
            shifted = from_behind(outgoing, "depth", 1)
        if sending:
            hits = (columns[None, :] == shot_node_indices[moment][:, None]).astype(jnp.float32)
            top_panel = emitted_pulse[0, moment][:, None, None] * hits[None]
            present_shot_matrix = jnp.where(at_surface, top_panel, shifted)
    gradient_out = lax.psum_scatter(gradient_sum[None, :], "freq", scatter_dimension=1, tiled=True)
    return (outgoing[None, None], gradient_out)


def solution(mesh):
    placed = (
        P("freq", "depth", None, None, None),
        P("depth", None),
        P("freq", "depth", None, None, None, None),
        P("freq", "depth", None, None, None),
        P(),
        P("freq", None, None),
    )
    return jax.shard_map(
        local,
        mesh=mesh,
        in_specs=placed,
        out_specs=(P("freq", "depth", None, None, None), P("depth", "freq")),
        check_vma=False,
    )
```

profile of v0, /device:TPU:24, one launch (start us, length us, event | category | flops | bytes accessed | tf_op | source)
XLA Modules:
  0.0 214.6 jit_solution(18310059619605966201)
XLA Ops:
  7.2 0.0 reduce-scatter.4.cloned.1.call-start
  7.2 1.3 fusion.68
  8.5 2.0 fusion.38
  10.5 0.7 fusion.22
  11.3 0.0 copy-start.5
  11.3 0.0 copy-start.4
  11.3 0.7 fusion.9
  12.1 0.7 fusion.8
  12.8 1.9 collective-permute-start
  14.8 0.2 slice_reduce_fusion.3
  15.0 0.1 fusion.73
  15.1 16.0 %collective-permute-done = f32[2,96,512]{2,1,0:T(8,128)S(1)} collective-permute-done((f32[2,96,512]{2,1,0:T(8,128)S(1)}, f32[2,96,512]{2,1,0:T(8,128)S(1)}, u32[]{:S(2)}, u32[]{:S(2)}) %collective-permute-start) | collective-permute-done | bytes 393248 | tf_op jit(solution)/shard_map/ppermute | solution.py:14
  31.1 1.1 fusion.66
  32.2 0.7 fusion.20
  32.9 0.7 fusion.34
  33.7 0.0 copy-start.1
  33.7 0.7 fusion.7
  34.4 0.7 fusion.6
  35.2 1.9 collective-permute-start.1
  37.2 0.1 fusion.72
  37.2 14.6 %collective-permute-done.1 = f32[2,96,512]{2,1,0:T(8,128)S(1)} collective-permute-done((f32[2,96,512]{2,1,0:T(8,128)S(1)}, f32[2,96,512]{2,1,0:T(8,128)S(1)}, u32[]{:S(2)}, u32[]{:S(2)}) %collective-permute-start.1) | collective-permute-done | bytes 393248 | tf_op jit(solution)/shard_map/ppermute | solution.py:14
  51.8 0.1 fusion.64
  52.0 0.7 fusion.17
  52.7 0.7 fusion.31
  53.5 0.7 fusion.5
  54.2 0.7 fusion.4
  55.0 1.9 collective-permute-start.2
  56.9 0.1 fusion.71
  57.0 14.6 %collective-permute-done.2 = f32[2,96,512]{2,1,0:T(8,128)S(1)} collective-permute-done((f32[2,96,512]{2,1,0:T(8,128)S(1)}, f32[2,96,512]{2,1,0:T(8,128)S(1)}, u32[]{:S(2)}, u32[]{:S(2)}) %collective-permute-start.2) | collective-permute-done | bytes 393248 | tf_op jit(solution)/shard_map/ppermute | solution.py:14
  71.6 0.1 fusion.62
  71.7 0.7 fusion.14
  72.5 0.7 fusion.28
  73.2 0.7 fusion.3
  74.0 0.7 fusion.2
  74.7 2.1 collective-permute-start.3
  76.9 0.1 fusion.70
  76.9 14.4 %collective-permute-done.3 = f32[2,96,512]{2,1,0:T(8,128)S(1)} collective-permute-done((f32[2,96,512]{2,1,0:T(8,128)S(1)}, f32[2,96,512]{2,1,0:T(8,128)S(1)}, u32[]{:S(2)}, u32[]{:S(2)}) %collective-permute-start.3) | collective-permute-done | bytes 393248 | tf_op jit(solution)/shard_map/ppermute | solution.py:14
  91.3 0.1 fusion.60
  91.5 0.7 fusion.11
  92.2 0.7 fusion.25
  93.0 0.6 fusion.67
  93.6 0.8 copy.8
  94.5 0.0 reduce-scatter.4.cloned.1.call-update
  94.5 0.7 fusion.1
  95.2 0.7 fusion
  96.0 0.8 maximum_bitcast_fusion
  96.7 109.7 %reduce-scatter.4.cloned.1.call-done = f32[64,1]{1,0:T(8,128)} async-done(((f32[512,1]{1,0:T(8,128)}), f32[64,1]{1,0:T(8,128)}) %reduce-scatter.4.cloned.1.call-update) | async-done | bytes 272
  206.4 1.3 copy.9
  (15 shorter events, 0.1 us)
Async XLA Ops:
  7.2 3.4 %copy-start = (f32[1,1,2,512,512]{4,3,2,1,0:T(8,128)S(1)}, f32[1,1,2,512,512]{4,3,2,1,0:T(8,128)}, u32[]{:S(2)}) copy-start(f32[1,1,2,512,512]{4,3,2,1,0:T(8,128)} %param.6) | copy-start | bytes 6291460
  7.2 199.2 %reduce-scatter.4.cloned.1.call-start = ((), (), s32[]{:S(2)}) async-start(), calls=%async_computation.1 | async-start | bytes 294912
  11.3 3.5 %copy-start.5 = (s32[4,96]{1,0:T(4,128)S(1)}, s32[4,96]{1,0:T(4,128)}, u32[]{:S(2)}) copy-start(s32[4,96]{1,0:T(4,128)} %param.10) | copy-start | bytes 4612
  11.3 3.5 %copy-start.4 = (f32[1,4,2]{1,2,0:T(2,128)S(1)}, f32[1,4,2]{1,2,0:T(2,128)}, u32[]{:S(2)}) copy-start(f32[1,4,2]{1,2,0:T(2,128)} %param.11) | copy-start | bytes 100
  11.3 19.8 %copy-start.3 = (f32[1,512]{1,0:T(1,128)S(1)}, f32[1,512]{1,0:T(1,128)}, u32[]{:S(2)}) copy-start(f32[1,512]{1,0:T(1,128)} %param.7) | copy-start | bytes 6148
  12.8 18.2 %collective-permute-start = (f32[2,96,512]{2,1,0:T(8,128)S(1)}, f32[2,96,512]{2,1,0:T(8,128)S(1)}, u32[]{:S(2)}, u32[]{:S(2)}) collective-permute-start(f32[2,96,512]{2,1,0:T(8,128)S(1)} %pad_maximum_fusion), channel_id=1, source_target_pairs={{0,8},{8,16},{16,24},{24,32},{32,40},{40,48},{48,56},{56,64},{64,7... | collective-permute-start | bytes 1179656 | tf_op jit(solution)/shard_map/ppermute | solution.py:14
  33.7 18.1 %copy-start.1 = (f32[1,1,5,2,96,512]{5,4,3,2,1,0:T(8,128)S(1)}, f32[1,1,5,2,96,512]{5,4,3,2,1,0:T(8,128)}, u32[]{:S(2)}) copy-start(f32[1,1,5,2,96,512]{5,4,3,2,1,0:T(8,128)} %param.8) | copy-start | bytes 5898244
  35.2 16.6 %collective-permute-start.1 = (f32[2,96,512]{2,1,0:T(8,128)S(1)}, f32[2,96,512]{2,1,0:T(8,128)S(1)}, u32[]{:S(2)}, u32[]{:S(2)}) collective-permute-start(f32[2,96,512]{2,1,0:T(8,128)S(1)} %pad_maximum_fusion.1), channel_id=1, source_target_pairs={{0,8},{8,16},{16,24},{24,32},{32,40},{40,48},{48,56},{56,64},{64,7... | collective-permute-start | bytes 1179656 | tf_op jit(solution)/shard_map/ppermute | solution.py:14
  55.0 16.6 %collective-permute-start.2 = (f32[2,96,512]{2,1,0:T(8,128)S(1)}, f32[2,96,512]{2,1,0:T(8,128)S(1)}, u32[]{:S(2)}, u32[]{:S(2)}) collective-permute-start(f32[2,96,512]{2,1,0:T(8,128)S(1)} %pad_maximum_fusion.2), channel_id=1, source_target_pairs={{0,8},{8,16},{16,24},{24,32},{32,40},{40,48},{48,56},{56,64},{64,7... | collective-permute-start | bytes 1179656 | tf_op jit(solution)/shard_map/ppermute | solution.py:14
  74.7 16.6 %collective-permute-start.3 = (f32[2,96,512]{2,1,0:T(8,128)S(1)}, f32[2,96,512]{2,1,0:T(8,128)S(1)}, u32[]{:S(2)}, u32[]{:S(2)}) collective-permute-start(f32[2,96,512]{2,1,0:T(8,128)S(1)} %pad_maximum_fusion.3), channel_id=1, source_target_pairs={{0,8},{8,16},{16,24},{24,32},{32,40},{40,48},{48,56},{56,64},{64,7... | collective-permute-start | bytes 1179656 | tf_op jit(solution)/shard_map/ppermute | solution.py:14
  91.3 1.6 copy-start.2
Sparse Core Ops, SparseCore 0:
  94.6 111.7 reduce-scatter.3
where the time goes:
time: 215 us
  waiting for transfers between devices  169 us (79%)
  matrix products  16.1 us (7%)
  between operations  14.3 us (7%)
  starting transfers between devices  7.9 us (4%)
  other arithmetic  4.69 us (2%)
  local copies, waits for them, and re-layouts  2.45 us (1%)
    unnamed x2, waiting for transfers between devices  110 us
    ppermute x4, waiting for transfers between devices, from_behind(): return lax.ppermute(block, axis, route)  59.5 us
    dot_general x20, matrix products, matmul_high(): jnp.dot(left, right, precision=lax.Precision.HIGHEST, preferred_element_t...  16.1 us
    ppermute x4, starting transfers between devices, from_behind(): return lax.ppermute(block, axis, route)  7.86 us
  transfers between devices with their start and end apart: 5, of which 5 were waited for; matrix products, arithmetic and copies ran while one was open for 1% of the time, Pallas kernels for 0%

commit v1 on v0

v1 whole, which is shorter than its diff:
```python
import functools
import math

import jax
import jax.numpy as jnp
from jax import lax
from jax.experimental import pallas as pl
from jax.experimental.pallas import tpu as pltpu
from jax.sharding import PartitionSpec as P

TICKS = 5
MESH = pl.DeviceIdType.MESH


def kernel(
    levels,
    rates,
    parts,
    prop_hbm,
    refl_hbm,
    asc_hbm,
    first_hbm,
    spots_hbm,
    pulse_hbm,
    leaving_ref,
    grad_ref,
    prop,
    high,
    low,
    refl,
    asc,
    arriving,
    outgoing,
    spots,
    pulse,
    total,
    shares,
    load_sem,
    send_sem,
    recv_sem,
    give_sem,
    take_sem,
):
    level = lax.axis_index("depth")
    rate = lax.axis_index("freq")
    shots, nodes = arriving.shape[2], arriving.shape[3]
    rows = shots // parts

    loads = [
        pltpu.make_async_copy(prop_hbm, prop, load_sem.at[0]),
        pltpu.make_async_copy(first_hbm, arriving.at[0], load_sem.at[1]),
        pltpu.make_async_copy(refl_hbm, refl, load_sem.at[2]),
        pltpu.make_async_copy(spots_hbm, spots, load_sem.at[3]),
        pltpu.make_async_copy(pulse_hbm, pulse, load_sem.at[4]),
    ]
    waves = [pltpu.make_async_copy(asc_hbm.at[t], asc.at[t], load_sem.at[5 + t]) for t in range(TICKS)]
    loads[0].start()
    loads[1].start()
    waves[0].start()
    for load in loads[2:]:
        load.start()
    for wave in waves[1:]:
        wave.start()

    barrier = pltpu.get_barrier_semaphore()

    @pl.when(level > 0)
    def _():
        pl.semaphore_signal(barrier, inc=1, device_id={"depth": level - 1}, device_id_type=MESH)

    for away in range(1, rates):
        pl.semaphore_signal(barrier, inc=1, device_id={"freq": lax.rem(rate + away, rates)}, device_id_type=MESH)

    for load in loads:
        load.wait()

    for part in range(2):
        whole = prop[part]
        top = whole.astype(jnp.bfloat16)
        high[:, part * nodes : (part + 1) * nodes] = top
        low[:, part * nodes : (part + 1) * nodes] = (whole - top.astype(jnp.float32)).astype(jnp.bfloat16)

    @pl.when(level == 0)
    def _():
        column = lax.broadcasted_iota(jnp.int32, (shots, nodes), 1)
        turned = jnp.transpose(spots[...].astype(jnp.float32)).astype(jnp.int32)
        for t in range(TICKS - 1):
            hit = (column == turned[:, t : t + 1]).astype(jnp.float32)
            arriving[t + 1, 0] = hit * pulse[t : t + 1, 0:1]
            arriving[t + 1, 1] = hit * pulse[t : t + 1, 1:2]

    @pl.when(level < levels - 1)
    def _():
        pl.semaphore_wait(barrier, rates)

    @pl.when(level == levels - 1)
    def _():
        pl.semaphore_wait(barrier, rates - 1)

    total[...] = jnp.zeros_like(total)

    def passing(t, c):
        return pltpu.make_async_remote_copy(
            src_ref=outgoing.at[t, :, pl.ds(c * rows, rows)],
            dst_ref=arriving.at[t + 1, :, pl.ds(c * rows, rows)],
            send_sem=send_sem.at[t, c],
            recv_sem=recv_sem.at[t, c],
            device_id={"depth": lax.rem(level + 1, levels)},
            device_id_type=MESH,
        )

    for t in range(TICKS):
        if t > 0:
            waves[t].wait()
        else:
            waves[0].wait()
        for c in range(parts):
            at = pl.ds(c * rows, rows)
            if t > 0:

                @pl.when(level > 0)
                def _():
                    passing(t - 1, c).wait_recv()

            here = arriving[t, :, at]
            rising = asc[t, :, at]
            total[...] += jnp.sum((here * rising).reshape(2 * rows // 8, 8, nodes), axis=0)
            mixed = (here + refl[...] * rising).reshape(2 * rows, nodes)
            top = mixed.astype(jnp.bfloat16)
            rest = (mixed - top.astype(jnp.float32)).astype(jnp.bfloat16)
            both = jnp.concatenate([top, rest], axis=0)
            wide = jnp.dot(both, high[...], preferred_element_type=jnp.float32)
            wide = wide[: 2 * rows] + wide[2 * rows :] + jnp.dot(top, low[...], preferred_element_type=jnp.float32)
            real = wide[:rows, :nodes] - wide[rows:, nodes:]
            imag = wide[:rows, nodes:] + wide[rows:, :nodes]
            if t < TICKS - 1:
                outgoing[t, 0, at] = real
                outgoing[t, 1, at] = imag

                @pl.when(level < levels - 1)
                def _():
                    passing(t, c).start()
            else:
                leaving_ref[0, at] = real
                leaving_ref[1, at] = imag

    half = nodes // rates
    per = 128 // half
    for tile in range(nodes // 128):
        shares[rates + tile] = total[:, tile * 128 : (tile + 1) * 128]

    def give(away):
        other = lax.rem(rate + away, rates)
        return pltpu.make_async_remote_copy(
            src_ref=shares.at[rates + other // per],
            dst_ref=shares.at[away],
            send_sem=give_sem.at[away],
            recv_sem=take_sem.at[away],
            device_id={"freq": other},
            device_id_type=MESH,
        )

    for away in range(1, rates):
        give(away).start()
    summed = shares[rates + rate // per]
    for away in range(1, rates):
        give(away).wait_recv()
        summed += shares[away]
    row = jnp.sum(summed, axis=0, keepdims=True) * (1.0 / math.sqrt(shots * TICKS))
    place = lax.rem(rate, per)
    mine = row[:, :half]
    for k in range(1, per):
        mine = jnp.where(place == k, row[:, k * half : (k + 1) * half], mine)
    grad_ref[...] = mine
    for away in range(1, rates):
        give(away).wait_send()

    @pl.when(level < levels - 1)
    def _():
        for t in range(TICKS - 1):
            for c in range(parts):
                passing(t, c).wait_send()


def local(levels, rates, prop, refl, asc, first, spots, pulse):
    shots, nodes = first.shape[3], first.shape[4]
    parts = 3
    prop = prop.reshape(2, nodes, nodes)
    asc = asc.reshape(TICKS, 2, shots, nodes)
    first = first.reshape(2, shots, nodes)
    pulse = pulse.reshape(TICKS - 1, 2)
    leaving, grad = pl.pallas_call(
        functools.partial(kernel, levels, rates, parts),
        out_shape=(
            jax.ShapeDtypeStruct((2, shots, nodes), jnp.float32),
            jax.ShapeDtypeStruct((1, nodes // rates), jnp.float32),
        ),
        in_specs=[pl.BlockSpec(memory_space=pl.ANY)] * 6,
        out_specs=(pl.BlockSpec(memory_space=pltpu.VMEM), pl.BlockSpec(memory_space=pltpu.VMEM)),
        scratch_shapes=[
            pltpu.VMEM((2, nodes, nodes), jnp.float32),
            pltpu.VMEM((nodes, 2 * nodes), jnp.bfloat16),
            pltpu.VMEM((nodes, 2 * nodes), jnp.bfloat16),
            pltpu.VMEM((1, nodes), jnp.float32),
            pltpu.VMEM((TICKS, 2, shots, nodes), jnp.float32),
            pltpu.VMEM((TICKS, 2, shots, nodes), jnp.float32),
            pltpu.VMEM((TICKS - 1, 2, shots, nodes), jnp.float32),
            pltpu.VMEM((TICKS - 1, shots), jnp.int32),
            pltpu.VMEM((TICKS - 1, 2), jnp.float32),
            pltpu.VMEM((8, nodes), jnp.float32),
            pltpu.VMEM((rates + nodes // 128, 8, 128), jnp.float32),
            pltpu.SemaphoreType.DMA((5 + TICKS,)),
            pltpu.SemaphoreType.DMA((TICKS - 1, parts)),
            pltpu.SemaphoreType.DMA((TICKS - 1, parts)),
            pltpu.SemaphoreType.DMA((rates,)),
            pltpu.SemaphoreType.DMA((rates,)),
        ],
        compiler_params=pltpu.CompilerParams(collective_id=0, has_side_effects=True, vmem_limit_bytes=48 << 20),
    )(prop, refl, asc, first, spots, pulse)
    return leaving[None, None], grad


def solution(mesh):
    placed = (
        P("freq", "depth", None, None, None),
        P("depth", None),
        P("freq", "depth", None, None, None, None),
        P("freq", "depth", None, None, None),
        P(),
        P("freq", None, None),
    )
    return jax.shard_map(
        functools.partial(local, mesh.shape["depth"], mesh.shape["freq"]),
        mesh=mesh,
        in_specs=placed,
        out_specs=(P("freq", "depth", None, None, None), P("depth", "freq")),
        check_vma=False,
    )
```

time: 215 us -> 57.5 us (0.27)
  waiting for transfers between devices: 169 us -> 0 us
  Pallas kernels: 0 us -> 49.1 us
  matrix products: 16.1 us -> 0 us
  between operations: 14.3 us -> 0.64 us
  starting transfers between devices: 7.9 us -> 0 us
  local copies, waits for them, and re-layouts: 2.45 us -> 7.52 us
  other arithmetic: 4.69 us -> 0 us
    unnamed x2 -> x0, waiting for transfers between devices: 110 us -> none
    ppermute x4 -> x0, waiting for transfers between devices: 59.5 us -> none  [from_behind(): return lax.ppermute(block, axis, route)]
    pallas_call x0 -> x1, Pallas kernels: none -> 49.1 us  [local(): pl.pallas_call(functools.partial(kernel, levels, rates, parts), out_shape...]
    dot_general x20 -> x0, matrix products: 16.1 us -> none  [matmul_high(): jnp.dot(left, right, precision=lax.Precision.HIGHEST, preferred_element_t...]
    ppermute x4 -> x0, starting transfers between devices: 7.86 us -> none  [from_behind(): return lax.ppermute(block, axis, route)]
    unnamed x14 -> x12, local copies, waits for them, and re-layouts: 2.23 us -> 6.75 us
    add x6 -> x0, other arithmetic: 2.85 us -> none  [the longest x5 2.84 us: local(): mixed = present_shot_matrix + reflect[None, None, :] * wave_now]
  transfers between devices with their start and end apart: 5 -> 0, of which waited for: 5 -> 0; matrix products, arithmetic and copies ran while one was open for 1% -> 0% of each run, Pallas kernels for 0% -> 0%
where the time goes in v1:
time: 57.5 us; the launch traced here: 57.2 us
  Pallas kernels  49.1 us (85%)
  local copies, waits for them, and re-layouts  7.52 us (13%)
  between operations  0.64 us (1%)
    pallas_call x1, Pallas kernels, local(): pl.pallas_call(functools.partial(kernel, levels, rates, parts), out_shape...  49.1 us
    unnamed x12, local copies, waits for them, and re-layouts  6.75 us

profile of v1, /device:TPU:24, one launch (start us, length us, event | category | flops | bytes accessed | tf_op | source)
XLA Modules:
  0.0 57.2 jit_solution(6284650786311098930)
XLA Ops:
  0.6 0.8 %copy.8.pulse_hbm = f32[4,2]{1,0:T(4,128)S(1)} copy(f32[4,2]{0,1:T(2,128)} %bitcast.9) | data formatting | bytes 64 | tf_op jit(solution)/shard_map/reshape | solution.py:191
  1.4 0.0 copy-start
  1.4 1.6 %copy-done = f32[1,1,2,512,512]{4,3,2,1,0:T(8,128)S(1)} copy-done((f32[1,1,2,512,512]{4,3,2,1,0:T(8,128)S(1)}, f32[1,1,2,512,512]{4,3,2,1,0:T(8,128)}, u32[]{:S(2)}) %copy-start) | copy-done | bytes 2097176
  3.0 0.0 copy-start.1
  3.0 1.5 %copy-done.1 = f32[1,1,5,2,96,512]{5,4,3,2,1,0:T(8,128)S(1)} copy-done((f32[1,1,5,2,96,512]{5,4,3,2,1,0:T(8,128)S(1)}, f32[1,1,5,2,96,512]{5,4,3,2,1,0:T(8,128)}, u32[]{:S(2)}) %copy-start.1) | copy-done | bytes 1966104
  4.5 0.0 copy-start.2
  4.5 1.0 %copy-done.2 = f32[1,1,2,96,512]{4,3,2,1,0:T(8,128)S(1)} copy-done((f32[1,1,2,96,512]{4,3,2,1,0:T(8,128)S(1)}, f32[1,1,2,96,512]{4,3,2,1,0:T(8,128)}, u32[]{:S(2)}) %copy-start.2) | copy-done | bytes 393240
  5.5 0.0 copy-start.3
  5.5 0.7 %copy-done.3 = f32[1,512]{1,0:T(1,128)S(1)} copy-done((f32[1,512]{1,0:T(1,128)S(1)}, f32[1,512]{1,0:T(1,128)}, u32[]{:S(2)}) %copy-start.3) | copy-done | bytes 2072
  6.2 0.0 copy-start.4
  6.2 0.7 %copy-done.4 = s32[4,96]{1,0:T(4,128)S(1)} copy-done((s32[4,96]{1,0:T(4,128)S(1)}, s32[4,96]{1,0:T(4,128)}, u32[]{:S(2)}) %copy-start.4) | copy-done | bytes 1560
  6.9 49.1 %shard_map.77 = (f32[2,96,512]{2,1,0:T(8,128)S(1)}, f32[1,64]{1,0:T(1,128)S(1)}) custom-call(f32[2,512,512]{2,1,0:T(8,128)S(1)} %bitcast.5, f32[1,512]{1,0:T(1,128)S(1)} %copy-done.3, f32[5,2,96,512]{3,2,1,0:T(8,128)S(1)} %bitcast.6, f32[2,96,512]{2,1,0:T(8,128)S(1)} %bitcast.7, s32[4,96]{1,0:T(4,128)S(1)} %copy-done.4, f32[4,2]{1,0:T(4,128)S(1)} %copy.8.pulse_hbm), custom_call_target="tpu_custom_call" | custom-call | tf_op jit(solution)/shard_map/pallas_call | solution.py:192
  56.0 0.7 %copy.11 = f32[1,1,2,96,512]{4,3,2,1,0:T(8,128)} copy(f32[1,1,2,96,512]{4,3,2,1,0:T(8,128)S(1)} %bitcast.8) | data formatting | bytes 786432
  56.7 0.5 copy.12
Async XLA Ops:
  1.4 1.6 %copy-start = (f32[1,1,2,512,512]{4,3,2,1,0:T(8,128)S(1)}, f32[1,1,2,512,512]{4,3,2,1,0:T(8,128)}, u32[]{:S(2)}) copy-start(f32[1,1,2,512,512]{4,3,2,1,0:T(8,128)} %param.6) | copy-start | bytes 6291460
  3.0 1.5 %copy-start.1 = (f32[1,1,5,2,96,512]{5,4,3,2,1,0:T(8,128)S(1)}, f32[1,1,5,2,96,512]{5,4,3,2,1,0:T(8,128)}, u32[]{:S(2)}) copy-start(f32[1,1,5,2,96,512]{5,4,3,2,1,0:T(8,128)} %param.8) | copy-start | bytes 5898244
  4.5 1.0 %copy-start.2 = (f32[1,1,2,96,512]{4,3,2,1,0:T(8,128)S(1)}, f32[1,1,2,96,512]{4,3,2,1,0:T(8,128)}, u32[]{:S(2)}) copy-start(f32[1,1,2,96,512]{4,3,2,1,0:T(8,128)} %param.9) | copy-start | bytes 1179652
  5.5 0.7 %copy-start.3 = (f32[1,512]{1,0:T(1,128)S(1)}, f32[1,512]{1,0:T(1,128)}, u32[]{:S(2)}) copy-start(f32[1,512]{1,0:T(1,128)} %refl_hbm.1) | copy-start | bytes 6148
  6.2 0.7 %copy-start.4 = (s32[4,96]{1,0:T(4,128)S(1)}, s32[4,96]{1,0:T(4,128)}, u32[]{:S(2)}) copy-start(s32[4,96]{1,0:T(4,128)} %spots_hbm.1) | copy-start | bytes 4612

commit v2 on v1

--- a/solution.py
+++ b/solution.py
@@ -21,7 +21,7 @@
     asc_hbm,
     first_hbm,
     spots_hbm,
-    pulse_hbm,
+    pulse,
     leaving_ref,
     grad_ref,
     prop,
@@ -32,7 +32,6 @@
     arriving,
     outgoing,
     spots,
-    pulse,
     total,
     shares,
     load_sem,
@@ -51,7 +50,6 @@
         pltpu.make_async_copy(first_hbm, arriving.at[0], load_sem.at[1]),
         pltpu.make_async_copy(refl_hbm, refl, load_sem.at[2]),
         pltpu.make_async_copy(spots_hbm, spots, load_sem.at[3]),
-        pltpu.make_async_copy(pulse_hbm, pulse, load_sem.at[4]),
     ]
     waves = [pltpu.make_async_copy(asc_hbm.at[t], asc.at[t], load_sem.at[5 + t]) for t in range(TICKS)]
     loads[0].start()
@@ -86,8 +84,8 @@
         turned = jnp.transpose(spots[...].astype(jnp.float32)).astype(jnp.int32)
         for t in range(TICKS - 1):
             hit = (column == turned[:, t : t + 1]).astype(jnp.float32)
-            arriving[t + 1, 0] = hit * pulse[t : t + 1, 0:1]
-            arriving[t + 1, 1] = hit * pulse[t : t + 1, 1:2]
+            arriving[t + 1, 0] = hit * pulse[0:1, t : t + 1]
+            arriving[t + 1, 1] = hit * pulse[1:2, t : t + 1]
 
     @pl.when(level < levels - 1)
     def _():
@@ -188,14 +186,14 @@
     prop = prop.reshape(2, nodes, nodes)
     asc = asc.reshape(TICKS, 2, shots, nodes)
     first = first.reshape(2, shots, nodes)
-    pulse = pulse.reshape(TICKS - 1, 2)
+    pulse = pulse.reshape(TICKS - 1, 2).T
     leaving, grad = pl.pallas_call(
         functools.partial(kernel, levels, rates, parts),
         out_shape=(
             jax.ShapeDtypeStruct((2, shots, nodes), jnp.float32),
             jax.ShapeDtypeStruct((1, nodes // rates), jnp.float32),
         ),
-        in_specs=[pl.BlockSpec(memory_space=pl.ANY)] * 6,
+        in_specs=[pl.BlockSpec(memory_space=pltpu.HBM)] * 5 + [pl.BlockSpec(memory_space=pltpu.VMEM)],
         out_specs=(pl.BlockSpec(memory_space=pltpu.VMEM), pl.BlockSpec(memory_space=pltpu.VMEM)),
         scratch_shapes=[
             pltpu.VMEM((2, nodes, nodes), jnp.float32),
@@ -206,7 +204,6 @@
             pltpu.VMEM((TICKS, 2, shots, nodes), jnp.float32),
             pltpu.VMEM((TICKS - 1, 2, shots, nodes), jnp.float32),
             pltpu.VMEM((TICKS - 1, shots), jnp.int32),
-            pltpu.VMEM((TICKS - 1, 2), jnp.float32),
             pltpu.VMEM((8, nodes), jnp.float32),
             pltpu.VMEM((rates + nodes // 128, 8, 128), jnp.float32),
             pltpu.SemaphoreType.DMA((5 + TICKS,)),
@@ -215,7 +212,7 @@
             pltpu.SemaphoreType.DMA((rates,)),
             pltpu.SemaphoreType.DMA((rates,)),
         ],
-        compiler_params=pltpu.CompilerParams(collective_id=0, has_side_effects=True, vmem_limit_bytes=48 << 20),
+        compiler_params=pltpu.CompilerParams(collective_id=0, has_side_effects=True),
     )(prop, refl, asc, first, spots, pulse)
     return leaving[None, None], grad
 

time: 57.5 us -> 52.9 us (0.920)
  local copies, waits for them, and re-layouts: 7.52 us -> 2.89 us
    unnamed x12 -> x2, local copies, waits for them, and re-layouts: 6.75 us -> 2.89 us
    reshape x1 -> x0, local copies, waits for them, and re-layouts: 0.77 us -> none  [local(): pulse = pulse.reshape(TICKS - 1, 2)]
where the time goes in v2:
time: 52.9 us; the launch traced here: 52.7 us
  Pallas kernels  49.2 us (93%)
  local copies, waits for them, and re-layouts  2.89 us (5%)
  between operations  0.64 us (1%)
    pallas_call x1, Pallas kernels, local(): pl.pallas_call(functools.partial(kernel, levels, rates, parts), out_shape...  49.2 us
    unnamed x2, local copies, waits for them, and re-layouts  2.89 us

profile of v2, /device:TPU:24, one launch (start us, length us, event | category | flops | bytes accessed | tf_op | source)
XLA Modules:
  0.0 52.7 jit_solution(14636697977031905704)
XLA Ops:
  0.6 49.2 %shard_map.77 = (f32[2,96,512]{2,1,0:T(8,128)}, f32[1,64]{1,0:T(1,128)}) custom-call(f32[2,512,512]{2,1,0:T(8,128)} %bitcast.7, f32[1,512]{1,0:T(1,128)} %refl_hbm.1, f32[5,2,96,512]{3,2,1,0:T(8,128)} %bitcast.8, f32[2,96,512]{2,1,0:T(8,128)} %bitcast.9, s32[4,96]{1,0:T(4,128)} %spots_hbm.1, f32[2,4]{1,0:T(2,128)} %bitcast.11), custom_call_target="tpu_custom_call" | custom-call | tf_op jit(solution)/shard_map/pallas_call | solution.py:190
  49.8 1.8 %copy.10 = f32[1,1,2,96,512]{4,3,2,1,0:T(8,128)} copy(f32[1,1,2,96,512]{4,3,2,1,0:T(8,128)} %bitcast.10) | data formatting | bytes 786432
  51.6 1.1 %copy.11 = f32[1,64]{1,0:T(1,128)} copy(f32[1,64]{1,0:T(1,128)} %get-tuple-element.9) | data formatting | bytes 512

commit v3 on v2

v3 whole, which is shorter than its diff:
```python
import functools
import math

import jax
import jax.numpy as jnp
from jax import lax
from jax.experimental import pallas as pl
from jax.experimental.pallas import tpu as pltpu
from jax.sharding import PartitionSpec as P

TICKS = 5
RUN = 16
PIECES = 4
MESH = pl.DeviceIdType.MESH


def kernel(
    levels,
    rates,
    parts,
    prop_hbm,
    refl_hbm,
    asc_hbm,
    first_hbm,
    spots_hbm,
    pulse,
    leaving_ref,
    grad_ref,
    prop,
    high,
    low,
    refl,
    asc,
    arriving,
    outgoing,
    passed,
    spots,
    total,
    shares,
    load_sem,
    wave_sem,
    block_sem,
    send_sem,
    recv_sem,
    give_sem,
    take_sem,
    go_sem,
    land_sem,
    onward_sem,
):
    level = lax.axis_index("depth")
    rate = lax.axis_index("freq")
    last = levels - 1
    shots, nodes = arriving.shape[2], arriving.shape[3]
    rows = shots // parts
    blocks = block_sem.shape[0]
    deep = nodes // blocks

    def block_load(k):
        return pltpu.make_async_copy(prop_hbm.at[:, pl.ds(k * deep, deep)], prop.at[:, pl.ds(k * deep, deep)], block_sem.at[k])

    def wave_load(t):
        return pltpu.make_async_copy(asc_hbm.at[t], asc.at[t], wave_sem.at[t])

    loads = [
        pltpu.make_async_copy(refl_hbm, refl, load_sem.at[0]),
        pltpu.make_async_copy(first_hbm, arriving.at[0], load_sem.at[1]),
        pltpu.make_async_copy(spots_hbm, spots, load_sem.at[2]),
    ]
    barrier = pltpu.get_barrier_semaphore()

    line, spot = level // RUN, lax.rem(level, RUN)
    lines = levels // RUN
    first = (spot == 0) & (level > 0)
    long = (spot == RUN - 1) & (level < last)
    near = (spot == RUN // 2) & (line < lines - 1)
    side = (spot == RUN - 2) & (line > 0)
    plain = (level < last) & (spot != RUN - 1)

    def ready(there):
        pl.semaphore_signal(barrier, inc=1, device_id={"depth": there}, device_id_type=MESH)

    @pl.when(spot > 0)
    def _():
        ready(level - 1)

    @pl.when(first)
    def _():
        ready(level - RUN // 2)
        ready(level + RUN - 2)

    @pl.when(near)
    def _():
        ready(level + RUN // 2 - 1)

    @pl.when(side)
    def _():
        ready(level - RUN + 1)

    for k in range(blocks):
        block_load(k).start()
    for load in loads:
        load.start()
    wave_load(0).start()

    home = lax.rem(level, rates)
    hub = level == last
    inside = hub & (home == rate)

    @pl.when(jnp.logical_not(inside))
    def _():
        pl.semaphore_signal(barrier, inc=1, device_id={"depth": last, "freq": home}, device_id_type=MESH)

    for k in range(blocks):
        block_load(k).wait()
        at = pl.ds(k * deep, deep)
        for part in range(2):
            whole = prop[part, at]
            top = whole.astype(jnp.bfloat16)
            high[at, part * nodes : (part + 1) * nodes] = top
            low[at, part * nodes : (part + 1) * nodes] = (whole - top.astype(jnp.float32)).astype(jnp.bfloat16)
    for load in loads:
        load.wait()
    wave_load(0).wait()
    for t in range(1, TICKS):
        wave_load(t).start()

    total[...] = jnp.zeros_like(total)

    def admit():
        @pl.when(level < last)
        def _():
            pl.semaphore_wait(barrier, 1 + jnp.where(long | near | side, 1, 0))

        @pl.when(hub)
        def _():
            pl.semaphore_wait(barrier, levels - jnp.where(inside, 1, 0))

            def release(i, carry):
                there, which = (i // rates) * rates + rate, lax.rem(i, rates)

                @pl.when(jnp.logical_or(there != level, which != rate))
                def _():
                    pl.semaphore_signal(go_sem, inc=1, device_id={"depth": there, "freq": which}, device_id_type=MESH)

                return carry

            lax.fori_loop(0, levels, release, 0)

    def passing(t, c):
        return pltpu.make_async_remote_copy(
            src_ref=outgoing.at[t, :, pl.ds(c * rows, rows)],
            dst_ref=arriving.at[t + 1, :, pl.ds(c * rows, rows)],
            send_sem=send_sem.at[t, c],
            recv_sem=recv_sem.at[t, c],
            device_id={"depth": lax.rem(level + 1, levels)},
            device_id_type=MESH,
        )

    size = rows // PIECES

    def share(which):
        return lines - 1 - which

    def piece(t, c, p):
        at = pl.ds(c * rows + p * size, size)
        return pltpu.make_async_remote_copy(
            src_ref=outgoing.at[t, :, at],
            dst_ref=passed.at[t, :, at],
            send_sem=send_sem.at[t, c],
            recv_sem=land_sem.at[t, c, p],
            device_id={"depth": jnp.where(long, jnp.where(p < share(line), level - RUN // 2 + 1, level + RUN - 1), level)},
            device_id_type=MESH,
        )

    def onward(t, c, p):
        at = pl.ds(c * rows + p * size, size)
        return pltpu.make_async_remote_copy(
            src_ref=passed.at[t, :, at],
            dst_ref=arriving.at[t + 1, :, at],
            send_sem=onward_sem.at[t, c, p],
            recv_sem=recv_sem.at[t, c],
            device_id={"depth": jnp.where(near, level + RUN // 2, jnp.where(side, level - RUN + 2, level))},
            device_id_type=MESH,
        )

    def carried(p):
        return (near & (p < share(line))) | (side & (p >= share(line - 1)))

    def send(t, c):
        @pl.when(plain)
        def _():
            passing(t, c).start()

        @pl.when(long)
        def _():
            for p in range(PIECES):
                piece(t, c, p).start()

    def relay(t, c):
        @pl.when(near | side)
        def _():
            for p in range(PIECES):

                @pl.when(carried(p))
                def _():
                    piece(t, c, p).wait_recv()
                    onward(t, c, p).start()

    def arrive(t, c):
        if t > 0:

            @pl.when(level > 0)
            def _():
                passing(t - 1, c).wait_recv()

    def correlate(t, c):
        at = pl.ds(c * rows, rows)
        total[...] += jnp.sum((arriving[t, :, at] * asc[t, :, at]).reshape(2 * rows // 8, 8, nodes), axis=0)

    def propagate(t, c):
        at = pl.ds(c * rows, rows)
        mixed = (arriving[t, :, at] + refl[...] * asc[t, :, at]).reshape(2 * rows, nodes)
        top = mixed.astype(jnp.bfloat16)
        rest = (mixed - top.astype(jnp.float32)).astype(jnp.bfloat16)
        both = jnp.concatenate([top, rest], axis=0)
        wide = jnp.dot(both, high[...], preferred_element_type=jnp.float32)
        wide = wide[: 2 * rows] + wide[2 * rows :] + jnp.dot(top, low[...], preferred_element_type=jnp.float32)
        result = outgoing.at[t] if t < TICKS - 1 else leaving_ref
        result[0, at] = wide[:rows, :nodes] - wide[rows:, nodes:]
        result[1, at] = wide[:rows, nodes:] + wide[rows:, :nodes]

    for c in range(parts):
        propagate(0, c)
        if c == 0:
            admit()
        send(0, c)
        correlate(0, c)

    for t in range(TICKS - 1):
        if t > 0:
            wave_load(t).wait()
        for c in range(parts if t > 0 else 0):
            arrive(t, c)
            propagate(t, c)
            send(t, c)
            correlate(t, c)
            if t == 1:
                relay(0, c)
            if t > 1:
                relay(t, c)
        if t == 1:
            for c in range(parts):
                relay(1, c)
        if t == 0:

            @pl.when(level == 0)
            def _():
                column = lax.broadcasted_iota(jnp.int32, (shots, nodes), 1)
                turned = jnp.transpose(spots[...].astype(jnp.float32)).astype(jnp.int32)
                for u in range(TICKS - 1):
                    hit = (column == turned[:, u : u + 1]).astype(jnp.float32)
                    arriving[u + 1, 0] = hit * pulse[0:1, u : u + 1]
                    arriving[u + 1, 1] = hit * pulse[1:2, u : u + 1]

    t = TICKS - 1
    wave_load(t).wait()
    for c in range(parts - 1):
        arrive(t, c)
        correlate(t, c)
        propagate(t, c)
    arrive(t, parts - 1)
    correlate(t, parts - 1)

    half = nodes // rates
    per = 128 // half
    for tile in range(nodes // 128):
        shares[rates + tile] = total[:, tile * 128 : (tile + 1) * 128]

    def give(away):
        other = lax.rem(rate + away, rates)
        return pltpu.make_async_remote_copy(
            src_ref=shares.at[rates + other // per],
            dst_ref=shares.at[away],
            send_sem=give_sem.at[away],
            recv_sem=take_sem.at[away],
            device_id={"freq": other},
            device_id_type=MESH,
        )

    @pl.when(jnp.logical_not(inside))
    def _():
        pl.semaphore_wait(go_sem, 1)

    for away in range(1, rates):
        give(away).start()

    propagate(t, parts - 1)

    @pl.when(level < last)
    def _():
        for u in range(TICKS - 1):
            for c in range(parts):
                passing(u, c).wait_send()

    @pl.when(near | side)
    def _():
        for p in range(PIECES):

            @pl.when(carried(p))
            def _():
                for u in range(TICKS - 1):
                    for c in range(parts):
                        onward(u, c, p).wait_send()

    summed = shares[rates + rate // per]
    for away in range(1, rates):
        give(away).wait_recv()
        summed += shares[away]
    row = jnp.sum(summed, axis=0, keepdims=True) * (1.0 / math.sqrt(shots * TICKS))
    place = lax.rem(rate, per)
    mine = row[:, :half]
    for k in range(1, per):
        mine = jnp.where(place == k, row[:, k * half : (k + 1) * half], mine)
    grad_ref[...] = mine
    for away in range(1, rates):
        give(away).wait_send()


def local(levels, rates, prop, refl, asc, first, spots, pulse):
    shots, nodes = first.shape[3], first.shape[4]
    parts = 3
    prop = prop.reshape(2, nodes, nodes)
    asc = asc.reshape(TICKS, 2, shots, nodes)
    first = first.reshape(2, shots, nodes)
    pulse = pulse.reshape(TICKS - 1, 2).T
    prop, refl, asc, first, spots, pulse = (pltpu.with_memory_space_constraint(x, pltpu.HBM) for x in (prop, refl, asc, first, spots, pulse))
    leaving, grad = pl.pallas_call(
        functools.partial(kernel, levels, rates, parts),
        out_shape=(
            jax.ShapeDtypeStruct((2, shots, nodes), jnp.float32),
            jax.ShapeDtypeStruct((1, nodes // rates), jnp.float32),
        ),
        in_specs=[pl.BlockSpec(memory_space=pltpu.HBM)] * 5 + [pl.BlockSpec(memory_space=pltpu.VMEM)],
        out_specs=(pl.BlockSpec(memory_space=pltpu.VMEM), pl.BlockSpec(memory_space=pltpu.VMEM)),
        scratch_shapes=[
            pltpu.VMEM((2, nodes, nodes), jnp.float32),
            pltpu.VMEM((nodes, 2 * nodes), jnp.bfloat16),
            pltpu.VMEM((nodes, 2 * nodes), jnp.bfloat16),
            pltpu.VMEM((1, nodes), jnp.float32),
            pltpu.VMEM((TICKS, 2, shots, nodes), jnp.float32),
            pltpu.VMEM((TICKS, 2, shots, nodes), jnp.float32),
            pltpu.VMEM((TICKS - 1, 2, shots, nodes), jnp.float32),
            pltpu.VMEM((TICKS - 1, 2, shots, nodes), jnp.float32),
            pltpu.VMEM((TICKS - 1, shots), jnp.int32),
            pltpu.VMEM((8, nodes), jnp.float32),
            pltpu.VMEM((rates + nodes // 128, 8, 128), jnp.float32),
            pltpu.SemaphoreType.DMA((3,)),
            pltpu.SemaphoreType.DMA((TICKS,)),
            pltpu.SemaphoreType.DMA((4,)),
            pltpu.SemaphoreType.DMA((TICKS - 1, parts)),
            pltpu.SemaphoreType.DMA((TICKS - 1, parts)),
            pltpu.SemaphoreType.DMA((rates,)),
            pltpu.SemaphoreType.DMA((rates,)),
            pltpu.SemaphoreType.REGULAR,
            pltpu.SemaphoreType.DMA((TICKS - 1, parts, PIECES)),
            pltpu.SemaphoreType.DMA((TICKS - 1, parts, PIECES)),
        ],
        compiler_params=pltpu.CompilerParams(collective_id=0, has_side_effects=True, vmem_limit_bytes=32 << 20),
    )(prop, refl, asc, first, spots, pulse)
    return leaving[None, None], grad


def solution(mesh):
    placed = (
        P("freq", "depth", None, None, None),
        P("depth", None),
        P("freq", "depth", None, None, None, None),
        P("freq", "depth", None, None, None),
        P(),
        P("freq", None, None),
    )
    return jax.shard_map(
        functools.partial(local, mesh.shape["depth"], mesh.shape["freq"]),
        mesh=mesh,
        in_specs=placed,
        out_specs=(P("freq", "depth", None, None, None), P("depth", "freq")),
        check_vma=False,
    )
```

time: 52.9 us -> 48.8 us (0.922)
  Pallas kernels: 49.2 us -> 46.7 us
  local copies, waits for them, and re-layouts: 2.89 us -> 1.26 us
    pallas_call x1, Pallas kernels: 49.2 us -> 46.7 us  [local(): pl.pallas_call(functools.partial(kernel, levels, rates, parts), out_shape...]
    unnamed x2, local copies, waits for them, and re-layouts: 2.89 us -> 1.26 us
where the time goes in v3:
time: 48.8 us; the launch traced here: 48.6 us
  Pallas kernels  46.7 us (96%)
  local copies, waits for them, and re-layouts  1.26 us (3%)
  between operations  0.64 us (1%)
    pallas_call x1, Pallas kernels, local(): pl.pallas_call(functools.partial(kernel, levels, rates, parts), out_shape...  46.7 us
    unnamed x2, local copies, waits for them, and re-layouts  1.26 us

profile of v3, /device:TPU:24, one launch (start us, length us, event | category | flops | bytes accessed | tf_op | source)
XLA Modules:
  0.0 48.6 jit_solution(2882953002421889062)
XLA Ops:
  0.6 46.7 %shard_map.77 = (f32[2,96,512]{2,1,0:T(8,128)S(1)}, f32[1,64]{1,0:T(1,128)S(1)}) custom-call(f32[2,512,512]{2,1,0:T(8,128)} %bitcast.8, f32[1,512]{1,0:T(1,128)} %refl_hbm.1, f32[5,2,96,512]{3,2,1,0:T(8,128)} %bitcast.9, f32[2,96,512]{2,1,0:T(8,128)} %bitcast.10, s32[4,96]{1,0:T(4,128)} %spots_hbm.1, f32[2,4]{1,0:T(2,128)} %bitcast.11), custom_call_target="tpu_custom_call" | custom-call | tf_op jit(solution)/shard_map/pallas_call | solution.py:338
  47.4 0.7 %copy.10 = f32[1,1,2,96,512]{4,3,2,1,0:T(8,128)} copy(f32[1,1,2,96,512]{4,3,2,1,0:T(8,128)S(1)} %bitcast.7) | data formatting | bytes 786432
  48.1 0.5 %copy.11 = f32[1,64]{1,0:T(1,128)} copy(f32[1,64]{1,0:T(1,128)S(1)} %get-tuple-element.9) | data formatting | bytes 512

commit v4 on v3

--- a/solution.py
+++ b/solution.py
@@ -10,6 +10,8 @@
 
 TICKS = 5
 RUN = 16
+NEAR = 10
+SHARES = ((4, 3, 2), (3, 2, 1), (3, 2, 1), (2, 1, 1))
 PIECES = 4
 MESH = pl.DeviceIdType.MESH
 
@@ -73,7 +75,7 @@
     lines = levels // RUN
     first = (spot == 0) & (level > 0)
     long = (spot == RUN - 1) & (level < last)
-    near = (spot == RUN // 2) & (line < lines - 1)
+    near = (spot == NEAR) & (line < lines - 1)
     side = (spot == RUN - 2) & (line > 0)
     plain = (level < last) & (spot != RUN - 1)
 
@@ -86,12 +88,12 @@
 
     @pl.when(first)
     def _():
-        ready(level - RUN // 2)
+        ready(level - RUN + NEAR)
         ready(level + RUN - 2)
 
     @pl.when(near)
     def _():
-        ready(level + RUN // 2 - 1)
+        ready(level + RUN - 1 - NEAR)
 
     @pl.when(side)
     def _():
@@ -159,8 +161,11 @@
 
     size = rows // PIECES
 
-    def share(which):
-        return lines - 1 - which
+    def share(which, t):
+        count = SHARES[t][0]
+        for k in range(1, lines - 1):
+            count = jnp.where(which == k, SHARES[t][k], count)
+        return count
 
     def piece(t, c, p):
         at = pl.ds(c * rows + p * size, size)
@@ -169,7 +174,7 @@
             dst_ref=passed.at[t, :, at],
             send_sem=send_sem.at[t, c],
             recv_sem=land_sem.at[t, c, p],
-            device_id={"depth": jnp.where(long, jnp.where(p < share(line), level - RUN // 2 + 1, level + RUN - 1), level)},
+            device_id={"depth": jnp.where(long, jnp.where(p < share(line, t), level - RUN + 1 + NEAR, level + RUN - 1), level)},
             device_id_type=MESH,
         )
 
@@ -180,12 +185,12 @@
             dst_ref=arriving.at[t + 1, :, at],
             send_sem=onward_sem.at[t, c, p],
             recv_sem=recv_sem.at[t, c],
-            device_id={"depth": jnp.where(near, level + RUN // 2, jnp.where(side, level - RUN + 2, level))},
+            device_id={"depth": jnp.where(near, level + RUN - NEAR, jnp.where(side, level - RUN + 2, level))},
             device_id_type=MESH,
         )
 
-    def carried(p):
-        return (near & (p < share(line))) | (side & (p >= share(line - 1)))
+    def carried(t, p):
+        return (near & (p < share(line, t))) | (side & (p >= share(line - 1, t)))
 
     def send(t, c):
         @pl.when(plain)
@@ -202,7 +207,7 @@
         def _():
             for p in range(PIECES):
 
-                @pl.when(carried(p))
+                @pl.when(carried(t, p))
                 def _():
                     piece(t, c, p).wait_recv()
                     onward(t, c, p).start()
@@ -241,12 +246,12 @@
         if t > 0:
             wave_load(t).wait()
         for c in range(parts if t > 0 else 0):
+            if t == 1:
+                relay(0, c)
             arrive(t, c)
             propagate(t, c)
             send(t, c)
             correlate(t, c)
-            if t == 1:
-                relay(0, c)
             if t > 1:
                 relay(t, c)
         if t == 1:
@@ -305,11 +310,11 @@
 
     @pl.when(near | side)
     def _():
-        for p in range(PIECES):
-
-            @pl.when(carried(p))
-            def _():
-                for u in range(TICKS - 1):
+        for u in range(TICKS - 1):
+            for p in range(PIECES):
+
+                @pl.when(carried(u, p))
+                def _():
                     for c in range(parts):
                         onward(u, c, p).wait_send()
 
@@ -325,6 +330,17 @@
     grad_ref[...] = mine
     for away in range(1, rates):
         give(away).wait_send()
+
+
+def deliver(panel_ref, row_ref, panel_out, row_out, sems):
+    copies = [
+        pltpu.make_async_copy(panel_ref, panel_out, sems.at[0]),
+        pltpu.make_async_copy(row_ref, row_out, sems.at[1]),
+    ]
+    for copy in copies:
+        copy.start()
+    for copy in copies:
+        copy.wait()
 
 
 def local(levels, rates, prop, refl, asc, first, spots, pulse):
@@ -368,6 +384,18 @@
         ],
         compiler_params=pltpu.CompilerParams(collective_id=0, has_side_effects=True, vmem_limit_bytes=32 << 20),
     )(prop, refl, asc, first, spots, pulse)
+    leaving, grad = pl.pallas_call(
+        deliver,
+        out_shape=(
+            jax.ShapeDtypeStruct(leaving.shape, jnp.float32),
+            jax.ShapeDtypeStruct(grad.shape, jnp.float32),
+        ),
+        in_specs=[pl.BlockSpec(memory_space=pltpu.VMEM)] * 2,
+        out_specs=(pl.BlockSpec(memory_space=pltpu.HBM), pl.BlockSpec(memory_space=pltpu.HBM)),
+        scratch_shapes=[pltpu.SemaphoreType.DMA((2,))],
+        compiler_params=pltpu.CompilerParams(vmem_limit_bytes=16 << 20),
+        name="deliver",
+    )(leaving, grad)
     return leaving[None, None], grad
 
 

time: 48.8 us -> 48.1 us (0.986)
  local copies, waits for them, and re-layouts: 1.26 us -> 0 us
  Pallas kernels: 46.7 us -> 47.2 us
    unnamed x2 -> x0, local copies, waits for them, and re-layouts: 1.26 us -> none
    pallas_call x0 -> x1, Pallas kernels: none -> 0.77 us  [local(): pl.pallas_call(deliver, out_shape=(jax.ShapeDtypeStruct(leaving.shape, jn...]
where the time goes in v4:
time: 48.1 us; the launch traced here: 47.9 us
  Pallas kernels  47.2 us (98%)
  between operations  0.64 us (1%)
    pallas_call x1, Pallas kernels, local(): pl.pallas_call(functools.partial(kernel, levels, rates, parts), out_shape...  46.5 us

profile of v4, /device:TPU:24, one launch (start us, length us, event | category | flops | bytes accessed | tf_op | source)
XLA Modules:
  0.0 47.9 jit_solution(7351500678638036477)
XLA Ops:
  0.6 46.5 %shard_map.77 = (f32[2,96,512]{2,1,0:T(8,128)S(1)}, f32[1,64]{1,0:T(1,128)S(1)}) custom-call(f32[2,512,512]{2,1,0:T(8,128)} %bitcast.7, f32[1,512]{1,0:T(1,128)} %refl_hbm.1, f32[5,2,96,512]{3,2,1,0:T(8,128)} %bitcast.8, f32[2,96,512]{2,1,0:T(8,128)} %bitcast.9, s32[4,96]{1,0:T(4,128)} %spots_hbm.1, f32[2,4]{1,0:T(2,128)} %bitcast.10), custom_call_target="tpu_custom_call" | custom-call | tf_op jit(solution)/shard_map/pallas_call | solution.py:354
  47.1 0.8 %deliver.1 = (f32[2,96,512]{2,1,0:T(8,128)}, f32[1,64]{1,0:T(1,128)}) custom-call(f32[2,96,512]{2,1,0:T(8,128)S(1)} %get-tuple-element.6.panel_ref, f32[1,64]{1,0:T(1,128)S(1)} %get-tuple-element.7.row_ref), custom_call_target="tpu_custom_call" | custom-call | tf_op jit(solution)/shard_map/deliver/pallas_call | solution.py:387

commit v5 on v4

--- a/solution.py
+++ b/solution.py
@@ -11,7 +11,7 @@
 TICKS = 5
 RUN = 16
 NEAR = 10
-SHARES = ((4, 3, 2), (3, 2, 1), (3, 2, 1), (2, 1, 1))
+SHARES = ((4, 3, 1), (3, 2, 1), (3, 2, 1), (2, 1, 1))
 PIECES = 4
 MESH = pl.DeviceIdType.MESH
 
@@ -297,7 +297,7 @@
     def _():
         pl.semaphore_wait(go_sem, 1)
 
-    for away in range(1, rates):
+    for away in (*range(1, rates, 2), *range(2, rates, 2)):
         give(away).start()
 
     propagate(t, parts - 1)

time: 48.1 us -> 48.1 us (level)
  no operation moved by 1% of the time
where the time goes in v5:
time: 48.1 us; the launch traced here: 47.9 us
  Pallas kernels  47.3 us (98%)
  between operations  0.64 us (1%)
    pallas_call x1, Pallas kernels, local(): pl.pallas_call(functools.partial(kernel, levels, rates, parts), out_shape...  46.5 us

profile of v5, /device:TPU:24, one launch (start us, length us, event | category | flops | bytes accessed | tf_op | source)
XLA Modules:
  0.0 47.9 jit_solution(3720037216890710953)
XLA Ops:
  0.6 46.5 %shard_map.77 = (f32[2,96,512]{2,1,0:T(8,128)S(1)}, f32[1,64]{1,0:T(1,128)S(1)}) custom-call(f32[2,512,512]{2,1,0:T(8,128)} %bitcast.7, f32[1,512]{1,0:T(1,128)} %refl_hbm.1, f32[5,2,96,512]{3,2,1,0:T(8,128)} %bitcast.8, f32[2,96,512]{2,1,0:T(8,128)} %bitcast.9, s32[4,96]{1,0:T(4,128)} %spots_hbm.1, f32[2,4]{1,0:T(2,128)} %bitcast.10), custom_call_target="tpu_custom_call" | custom-call | tf_op jit(solution)/shard_map/pallas_call | solution.py:354
  47.1 0.8 %deliver.1 = (f32[2,96,512]{2,1,0:T(8,128)}, f32[1,64]{1,0:T(1,128)}) custom-call(f32[2,96,512]{2,1,0:T(8,128)S(1)} %get-tuple-element.6.panel_ref, f32[1,64]{1,0:T(1,128)S(1)} %get-tuple-element.7.row_ref), custom_call_target="tpu_custom_call" | custom-call | tf_op jit(solution)/shard_map/deliver/pallas_call | solution.py:387
